TPU v7x, 32 devices: a whole 2x2x4 slice. The times are simulated.
32 devices in a mesh: rows: 8 (over z, y), sub: 4 (over x, core).
Axes of the slice: x: 2, y: 2, z: 4, core: 2. Of those that a mesh axis runs over, the one named last changes fastest.
Arguments:
- stiffness_tiles: bfloat16 [8, 4, 128, 128, 128], P('rows', 'sub'), may hold values from -0.5 to 0.5
- damping_tiles: bfloat16 [8, 4, 128, 128, 128], P('rows', 'sub'), may hold values from -0.5 to 0.5
- tile_map: int32 [8, 4, 2, 128], P('rows', 'sub'), may hold values from -1 to 767, as said below
- inv_mass: float32 [262144], P(('rows', 'sub')), may hold values from 0.5 to 2
- spectral_shift: float32 [], replicated, may hold values from 0.5 to 1.5
- basis: float32 [58, 262144], P(None, ('rows', 'sub')), may hold values from -20 to 20
- compact: float32 [2, 58, 57], replicated, may hold values from -0.54 to 0.54
Outputs:
- new_basis: float32 [2, 262144], P(None, ('rows', 'sub'))
- compact_out: float32 [2, 60, 59], replicated
- hessenberg: float32 [59, 2], replicated
Inputs may be any that keep to these rules, and one draw needn't show every extreme that they name: tile_map[r, s, 0, t] is the tile row of part r that slot t adds to, or -1 for an unused slot; the used slots of a device come first, and some device uses all 128. tile_map[r, s, 1, t] is the source column tile counted from the start of part r - 1.
All inputs are finite; a program needn't handle non-finite values.
Results may differ from a plain program's by a relative error of at most 0.0033.
Values may be sent and summed in bfloat16 or wider, within the bound.
No kernel may reach another device: no remote copies, remote signals or barrier semaphores. Data moves between devices by JAX's collectives and lax.ppermute only.
A program may use at most 64 MiB of HBM per device.

v0:
```python
import jax
import jax.numpy as jnp
from jax import lax
from jax.sharding import PartitionSpec as P

ITERS = 2
precise = lax.Precision.HIGHEST


def padded(array, sides, width):
    for axis, dim in sides:
        devices, length = (lax.axis_size(axis), array.shape[dim])
        up = [(i, (i + 1) % devices) for i in range(devices - 1)]
        down = [(j, i) for i, j in up]
        last = lax.slice_in_dim(array, length - width, length, axis=dim)
        initial = lax.slice_in_dim(array, 0, width, axis=dim)
        before = lax.ppermute(last, axis, up)
        after = lax.ppermute(initial, axis, down)
        array = jnp.concatenate([before, array, after], axis=dim)
    return array


def compact_update(upper_half, lower_half, coefficients, norm_value, lower_tail):
    columns = upper_half.shape[1]
    zero_row = jnp.zeros((1, columns), upper_half.dtype)
    upper_ext = jnp.concatenate([upper_half, zero_row], 0)
    lower_ext = jnp.concatenate([lower_half, zero_row], 0)
    upper_coeffs = jnp.concatenate([coefficients, norm_value[None]])
    lower_coeffs = jnp.concatenate([lower_tail, jnp.zeros((1,), lower_tail.dtype)])
    weights = jnp.zeros((columns,), upper_half.dtype)
    for repeat_index in range(2):
        projection = jnp.dot(upper_coeffs, upper_ext, precision=precise) + jnp.dot(
            lower_coeffs, lower_ext, precision=precise
        )
        upper_coeffs = upper_coeffs - jnp.dot(upper_ext, projection, precision=precise)
        lower_coeffs = lower_coeffs - jnp.dot(lower_ext, projection, precision=precise)
        weights = weights + projection
    beta_norm = jnp.sqrt(
        jnp.sum(upper_coeffs * upper_coeffs) + jnp.sum(lower_coeffs * lower_coeffs) + 1e-06
    )
    upper_new = jnp.concatenate([upper_ext, (upper_coeffs / beta_norm)[:, None]], 1)
    lower_new = jnp.concatenate([lower_ext, (lower_coeffs / beta_norm)[:, None]], 1)
    return (upper_new, lower_new, weights, beta_norm)


def tile_products(damping, stiffness, target, source, blocked, tile_rows):
    picked_damp = blocked[0][source]
    picked_stiff = blocked[1][source]
    product = jnp.einsum("sij,sj->si", damping, picked_damp, preferred_element_type=jnp.float32)
    product = product + jnp.einsum(
        "sij,sj->si", stiffness, picked_stiff, preferred_element_type=jnp.float32
    )
    selector = (target[None, :] == jnp.arange(tile_rows, dtype=jnp.int32)[:, None]).astype(
        jnp.float32
    )
    return jnp.dot(selector, product, precision=precise)


def on_device(stiffness_tiles, damping_tiles, tile_map, inv_mass, spectral_shift, basis, compact):
    rows_count = lax.axis_size("rows")
    sub_count = lax.axis_size("sub")
    tile_size = stiffness_tiles.shape[-1]
    local_rows = basis.shape[1]
    part_rows = sub_count * local_rows
    tile_rows = part_rows // tile_size
    unknowns = local_rows * rows_count * sub_count
    target = tile_map[0, 0, 0]
    source = tile_map[0, 0, 1]
    damping = damping_tiles[0, 0]
    stiffness = stiffness_tiles[0, 0]
    held = basis
    upper_half = compact[0]
    lower_half = compact[1]
    new_columns = []
    hess_columns = []
    for iteration in range(ITERS):
        upper_last = upper_half[:, -1]
        lower_last = lower_half[:, -1]
        upper_vec = jnp.dot(upper_last, held, precision=precise)
        lower_vec = jnp.dot(lower_last, held, precision=precise)
        vectors = jnp.stack([upper_vec, lower_vec]).astype(jnp.bfloat16)
        whole_part = lax.all_gather(vectors, "sub", axis=1, tiled=True)
        window = padded(whole_part, (("rows", 1),), part_rows)
        blocked = window.reshape(2, 3 * tile_rows, tile_size)
        summed = tile_products(damping, stiffness, target, source, blocked, tile_rows)
        partial_value = summed.reshape(-1)
        coupled = lax.psum_scatter(partial_value, "sub", scatter_dimension=0, tiled=True)
        image = spectral_shift * upper_vec - inv_mass * coupled
        image_inner, image_self, gram = lax.psum(
            (
                jnp.dot(held, image, precision=precise),
                jnp.sum(image * image),
                jnp.dot(held, held.T, precision=precise),
            ),
            ("rows", "sub"),
        )
        first_part = image_inner / unknowns
        gram = gram / unknowns
        second_part = first_part - jnp.dot(gram, first_part, precision=precise)
        coefficients = first_part + second_part
        residual_two = image - jnp.dot(coefficients, held, precision=precise)
        square_mean = (
            image_self / unknowns
            - 2.0 * jnp.dot(coefficients, first_part, precision=precise)
            + jnp.dot(
                coefficients, jnp.dot(gram, coefficients, precision=precise), precision=precise
            )
        )
        norm_value = jnp.sqrt(square_mean + 1e-06)
        column = residual_two / norm_value
        lower_tail = upper_last + spectral_shift * lower_last
        upper_half, lower_half, weights, beta_norm = compact_update(
            upper_half, lower_half, coefficients, norm_value, lower_tail
        )
        held = jnp.concatenate([held, column[None]], 0)
        new_columns.append(column)
        hess_columns.append(
            jnp.concatenate(
                [weights, beta_norm[None], jnp.zeros((ITERS - 1 - iteration,), weights.dtype)]
            )
        )
    return (
        jnp.stack(new_columns),
        jnp.stack([upper_half, lower_half]),
        jnp.stack(hess_columns, axis=1),
    )


def solution(mesh):
    in_specs = (
        P("rows", "sub", None, None, None),
        P("rows", "sub", None, None, None),
        P("rows", "sub", None, None),
        P(("rows", "sub")),
        P(),
        P(None, ("rows", "sub")),
        P(),
    )
    out_specs = (P(None, ("rows", "sub")), P(), P())
    return jax.shard_map(
        on_device, mesh=mesh, in_specs=in_specs, out_specs=out_specs, check_vma=False
    )
```

profile of v0, /device:TPU:0, one launch (start us, length us, event | category | flops | bytes accessed | tf_op | source)
XLA Modules:
  0.0 251.9 jit_solution(1315669255677280857)
XLA Ops:
  7.2 1.0 fusion.104
  8.5 0.2 slice_reduce_fusion.4
  8.7 2.7 %fusion.54 = f32[1,8192]{1,0:T(1,128)S(1)} fusion(f32[58,8192]{1,0:T(8,128)} %param.12, f32[58]{0:T(128)S(1)} %get-tuple-element.48), kind=kOutput, calls=%fused_computation.120 | convolution fusion | flops 5701632 | bytes 1933544 | tf_op jit(solution)/shard_map/dot_general | solution.py:79
  11.4 1.1 fusion.52
  12.6 6.5 %all_gather.6 = bf16[2,32768]{1,0:T(2,128)(2,1)S(1)} all-gather(bf16[2,8192]{1,0:T(2,128)(2,1)S(1)} %pad_maximum_fusion.8), channel_id=1, replica_groups=mesh['rows'=8,'sub'=4] {'sub'}, dimensions={1}, use_global_device_ids=true | all-gather | bytes 163840 | tf_op jit(solution)/shard_map/all_gather | solution.py:82
  19.1 3.9 %collective-permute-start = (bf16[2,32768]{1,0:T(2,128)(2,1)S(1)}, bf16[2,32768]{1,0:T(2,128)(2,1)S(1)}, u32[]{:S(2)}, u32[]{:S(2)}) collective-permute-start(bf16[2,32768]{1,0:T(2,128)(2,1)S(1)} %all_gather.6), channel_id=1, source_target_pairs={{0,4},{4,8},{8,12},{12,16},{16,20},{20,24},{24,28},{1,5},{5,9},{9,... | collective-permute-start | bytes 393224 | tf_op jit(solution)/shard_map/ppermute | solution.py:17
  23.1 1.3 collective-permute-start.1
  24.4 1.8 fusion.115
  26.9 0.1 constant_dynamic-update-slice_fusion.1
  27.1 3.4 %collective-permute-done.1 = bf16[2,32768]{1,0:T(2,128)(2,1)S(1)} collective-permute-done((bf16[2,32768]{1,0:T(2,128)(2,1)S(1)}, bf16[2,32768]{1,0:T(2,128)(2,1)S(1)}, u32[]{:S(2)}, u32[]{:S(2)}) %collective-permute-start.1) | collective-permute-done | bytes 131104 | tf_op jit(solution)/shard_map/ppermute | solution.py:18
  30.5 2.1 slice_reduce_fusion.2
  32.6 0.7 gather_fusion
  33.3 0.7 gather_fusion.1
  34.0 4.6 %fusion.6 = f32[128,1,128]{2,1,0:T(1,128)S(1)} fusion(bf16[1,1,128,128,128]{4,3,2,1,0:T(8,128)(2,1)} %param.8, bf16[128,128,1]{1,0,2:T(8,128)(2,1)S(1)} %bitcast.283), kind=kOutput, calls=%fused_computation.12 | convolution fusion | flops 4194304 | bytes 4292608 | tf_op jit(solution)/shard_map/sij,sj->si/dot_general | solution.py:49
  38.6 2.3 fusion.2
  40.9 0.9 convolution_bitcast_fusion.1
  41.9 0.6 dynamic-slice
  43.2 31.7 %all-reduce.11.cloned.1.call-done = f32[32768]{0:T(1024)} async-done(((f32[32768]{0:T(1024)}), f32[32768]{0:T(1024)}) %all-reduce.11.cloned.1.call-update) | async-done | bytes 131088
  74.9 1.4 multiply_reduce_fusion.1
  76.3 1.7 convolution_bitcast_fusion.23
  78.0 39.9 %all-reduce.7 = (f32[58,58]{1,0:T(8,128)S(1)}, f32[58]{0:T(128)S(1)}, f32[]{:T(128)}) all-reduce(f32[58,58]{1,0:T(8,128)S(1)} %fusion.115, f32[58]{0:T(128)S(1)} %convolution_bitcast_fusion.23, f32[]{:T(128)} %get-tuple-element.27), channel_id=1, replica_groups=mesh['rows'=8,'sub'=4] {'rows','sub'}, use_global_device_ids=true, to_apply=%region_2.0 | all-reduce | flops 3423 | bytes 27384 | tf_op jit(solution)/shard_map/psum | solution.py:89
  117.9 0.8 multiply_reduce_fusion.3
  118.7 0.8 fusion.26
  121.4 0.2 convolution_bitcast_fusion.19
  121.6 0.2 fusion.22
  121.8 0.2 fusion.20
  122.0 0.2 fusion.21
  122.2 0.2 convolution_bitcast_fusion.16
  122.3 0.1 fusion.106
  122.5 0.8 multiply_reduce_fusion.6
  123.3 0.8 multiply_reduce_fusion.7
  124.0 1.1 fusion.76
  126.5 1.1 fusion.31
  127.7 1.1 fusion.30
  129.0 5.8 %all_gather.7 = bf16[2,32768]{1,0:T(2,128)(2,1)S(1)} all-gather(bf16[2,8192]{1,0:T(2,128)(2,1)S(1)} %pad_maximum_fusion.9), channel_id=1, replica_groups=mesh['rows'=8,'sub'=4] {'sub'}, dimensions={1}, use_global_device_ids=true | all-gather | bytes 163840 | tf_op jit(solution)/shard_map/all_gather | solution.py:82
  134.8 3.8 %collective-permute-start.2 = (bf16[2,32768]{1,0:T(2,128)(2,1)S(1)}, bf16[2,32768]{1,0:T(2,128)(2,1)S(1)}, u32[]{:S(2)}, u32[]{:S(2)}) collective-permute-start(bf16[2,32768]{1,0:T(2,128)(2,1)S(1)} %all_gather.7), channel_id=1, source_target_pairs={{0,4},{4,8},{8,12},{12,16},{16,20},{20,24},{24,28},{1,5},{5,9},{9,... | collective-permute-start | bytes 393224 | tf_op jit(solution)/shard_map/ppermute | solution.py:17
  138.6 1.3 collective-permute-start.3
  139.9 1.8 fusion.29
  142.1 0.1 constant_dynamic-update-slice_fusion.4
  142.3 3.7 %collective-permute-done.3 = bf16[2,32768]{1,0:T(2,128)(2,1)S(1)} collective-permute-done((bf16[2,32768]{1,0:T(2,128)(2,1)S(1)}, bf16[2,32768]{1,0:T(2,128)(2,1)S(1)}, u32[]{:S(2)}, u32[]{:S(2)}) %collective-permute-start.3) | collective-permute-done | bytes 131104 | tf_op jit(solution)/shard_map/ppermute | solution.py:18
  146.0 2.1 slice_reduce_fusion
  148.1 0.7 gather_fusion.3
  148.8 4.4 %fusion = f32[128,1,128]{2,1,0:T(1,128)S(1)} fusion(bf16[1,1,128,128,128]{4,3,2,1,0:T(8,128)(2,1)} %param.7, bf16[128,128,1]{1,0,2:T(8,128)(2,1)S(1)} %bitcast.286), kind=kOutput, calls=%fused_computation.6 | convolution fusion | flops 4194304 | bytes 4292608 | tf_op jit(solution)/shard_map/sij,sj->si/dot_general | solution.py:50
  153.3 0.7 gather_fusion.2
  154.0 4.4 %fusion.4 = f32[128,1,128]{2,1,0:T(1,128)S(1)} fusion(bf16[1,1,128,128,128]{4,3,2,1,0:T(8,128)(2,1)} %param.8, bf16[128,128,1]{1,0,2:T(8,128)(2,1)S(1)} %bitcast.285), kind=kOutput, calls=%fused_computation.10 | convolution fusion | flops 4194304 | bytes 4292608 | tf_op jit(solution)/shard_map/sij,sj->si/dot_general | solution.py:49
  158.4 0.9 convolution_bitcast_fusion
  159.4 31.7 %all-reduce.13.cloned.1.call-done = f32[32768]{0:T(1024)} async-done(((f32[32768]{0:T(1024)}), f32[32768]{0:T(1024)}) %all-reduce.13.cloned.1.call-update) | async-done | bytes 131088
  191.1 1.4 multiply_reduce_fusion
  192.5 1.7 convolution_bitcast_fusion.22
  194.2 39.7 %all-reduce.6 = (f32[59,59]{1,0:T(8,128)S(1)}, f32[59]{0:T(128)S(1)}, f32[]{:T(128)}) all-reduce(f32[59,59]{1,0:T(8,128)S(1)} %fusion.29, f32[59]{0:T(128)S(1)} %convolution_bitcast_fusion.22, f32[]{:T(128)} %get-tuple-element.25), channel_id=1, replica_groups=mesh['rows'=8,'sub'=4] {'rows','sub'}, use_global_device_ids=true, to_apply=%region_9.0 | all-reduce | flops 3541 | bytes 28328 | tf_op jit(solution)/shard_map/psum | solution.py:89
  233.9 0.8 multiply_reduce_fusion.2
  234.7 0.8 fusion.27
  237.5 0.2 convolution_bitcast_fusion.9
  237.7 0.2 fusion.13
  237.9 0.2 fusion.12
  238.0 0.2 fusion.11
  238.2 0.2 convolution_bitcast_fusion.6
  238.4 0.1 fusion.105
  238.5 0.8 multiply_reduce_fusion.5
  239.3 0.8 multiply_reduce_fusion.4
  240.1 1.1 fusion.28
  243.0 0.7 copy.32
  243.7 0.7 pad_maximum_fusion.6
  244.5 0.6 pad_maximum_fusion.10
  (54 shorter events, 2.0 us)
Async XLA Ops:
  7.2 4.2 %copy-start = (f32[58,8192]{1,0:T(8,128)S(1)}, f32[58,8192]{1,0:T(8,128)}, u32[]{:S(2)}) copy-start(f32[58,8192]{1,0:T(8,128)} %param.12) | copy-start | bytes 5701636
  7.2 67.7 %all-reduce.11.cloned.1.call-start = ((), (), s32[]{:S(2)}) async-start(), calls=%async_computation | async-start | bytes 262144
  19.1 7.0 %copy-start.3 = (s32[1,1,2,128]{3,2,1,0:T(2,128)S(1)}, s32[1,1,2,128]{3,2,1,0:T(2,128)}, u32[]{:S(2)}) copy-start(s32[1,1,2,128]{3,2,1,0:T(2,128)} %param.9) | copy-start | bytes 3076
  19.1 7.7 %collective-permute-start = (bf16[2,32768]{1,0:T(2,128)(2,1)S(1)}, bf16[2,32768]{1,0:T(2,128)(2,1)S(1)}, u32[]{:S(2)}, u32[]{:S(2)}) collective-permute-start(bf16[2,32768]{1,0:T(2,128)(2,1)S(1)} %all_gather.6), channel_id=1, source_target_pairs={{0,4},{4,8},{8,12},{12,16},{16,20},{20,24},{24,28},{1,5},{5,9},{9,... | collective-permute-start | bytes 393224 | tf_op jit(solution)/shard_map/ppermute | solution.py:17
  23.1 7.4 %collective-permute-start.1 = (bf16[2,32768]{1,0:T(2,128)(2,1)S(1)}, bf16[2,32768]{1,0:T(2,128)(2,1)S(1)}, u32[]{:S(2)}, u32[]{:S(2)}) collective-permute-start(bf16[2,32768]{1,0:T(2,128)(2,1)S(1)} %all_gather.6), channel_id=1, source_target_pairs={{4,0},{8,4},{12,8},{16,12},{20,16},{24,20},{28,24},{5,1},{9,5},{13... | collective-permute-start | bytes 393224 | tf_op jit(solution)/shard_map/ppermute | solution.py:18
  34.0 4.6 %copy-start.1 = (bf16[1,1,128,128,128]{4,3,2,1,0:T(8,128)(2,1)S(1)}, bf16[1,1,128,128,128]{4,3,2,1,0:T(8,128)(2,1)}, u32[]{:S(2)}) copy-start(bf16[1,1,128,128,128]{4,3,2,1,0:T(8,128)(2,1)} %param.7) | copy-start | bytes 12582916
  38.6 3.3 %copy-start.4 = (u32[32]{0:T(128)S(1)}, u32[32]{0:T(128)}, u32[]{:S(2)}) copy-start(u32[32]{0:T(128)} %constant.43) | copy-start | bytes 388
  38.6 36.3 %copy-start.2 = (f32[8192]{0:T(1024)S(1)}, f32[8192]{0:T(1024)}, u32[]{:S(2)}) copy-start(f32[8192]{0:T(1024)} %param.10) | copy-start | bytes 98308
  41.8 149.3 %all-reduce.13.cloned.1.call-start = ((), (), s32[]{:S(2)}) async-start(), calls=%async_computation.1 | async-start | bytes 262144
  134.8 7.2 %collective-permute-start.2 = (bf16[2,32768]{1,0:T(2,128)(2,1)S(1)}, bf16[2,32768]{1,0:T(2,128)(2,1)S(1)}, u32[]{:S(2)}, u32[]{:S(2)}) collective-permute-start(bf16[2,32768]{1,0:T(2,128)(2,1)S(1)} %all_gather.7), channel_id=1, source_target_pairs={{0,4},{4,8},{8,12},{12,16},{16,20},{20,24},{24,28},{1,5},{5,9},{9,... | collective-permute-start | bytes 393224 | tf_op jit(solution)/shard_map/ppermute | solution.py:17
  138.6 7.4 %collective-permute-start.3 = (bf16[2,32768]{1,0:T(2,128)(2,1)S(1)}, bf16[2,32768]{1,0:T(2,128)(2,1)S(1)}, u32[]{:S(2)}, u32[]{:S(2)}) collective-permute-start(bf16[2,32768]{1,0:T(2,128)(2,1)S(1)} %all_gather.7), channel_id=1, source_target_pairs={{4,0},{8,4},{12,8},{16,12},{20,16},{24,20},{28,24},{5,1},{9,5},{13... | collective-permute-start | bytes 393224 | tf_op jit(solution)/shard_map/ppermute | solution.py:18
Sparse Core Ops, SparseCore 0:
  41.9 32.9 all-reduce.10
  159.5 31.5 all-reduce.12
where the time goes:
time: 253 us; the launch traced here: 252 us
  blocking collectives  91.9 us (36%)
  waiting for transfers between devices  70.5 us (28%)
  matrix products  41.1 us (16%)
  between operations  22.3 us (9%)
  local copies, waits for them, and re-layouts  10.9 us (4%)
  starting transfers between devices  10.4 us (4%)
  other arithmetic  4.73 us (2%)
    psum x2, blocking collectives, on_device(): lax.psum((jnp.dot(held, image, precision=precise), jnp.sum(image * image)...  79.6 us
    unnamed x4, waiting for transfers between devices  63.4 us
    all_gather x2, blocking collectives, on_device(): whole_part = lax.all_gather(vectors, 'sub', axis=1, tiled=True)  12.3 us
    dot_general x2, matrix products, tile_products(): jnp.einsum('sij,sj->si', damping, picked_damp, preferred_element_type=jnp...  9.01 us
    ppermute x2, starting transfers between devices, padded(): before = lax.ppermute(last, axis, up)  7.71 us
    ppermute x2, waiting for transfers between devices, padded(): after = lax.ppermute(initial, axis, down)  7.03 us
    dot_general x2, matrix products, tile_products(): jnp.einsum('sij,sj->si', stiffness, picked_stiff, preferred_element_type=...  6.71 us
  transfers between devices with their start and end apart: 6, of which 4 were waited for; matrix products, arithmetic and copies ran while one was open for 2% of the time, Pallas kernels for 0%

commit v1 on v0

--- a/solution.py
+++ b/solution.py
@@ -5,6 +5,11 @@
 
 ITERS = 2
 precise = lax.Precision.HIGHEST
+
+
+def by_each_axis(array_2, one, other):
+    half = lax.psum(array_2, one)
+    return lax.psum(half, other)
 
 
 def padded(array, sides, width):
@@ -86,13 +91,14 @@
         partial_value = summed.reshape(-1)
         coupled = lax.psum_scatter(partial_value, "sub", scatter_dimension=0, tiled=True)
         image = spectral_shift * upper_vec - inv_mass * coupled
-        image_inner, image_self, gram = lax.psum(
+        image_inner, image_self, gram = by_each_axis(
             (
                 jnp.dot(held, image, precision=precise),
                 jnp.sum(image * image),
                 jnp.dot(held, held.T, precision=precise),
             ),
-            ("rows", "sub"),
+            "sub",
+            "rows",
         )
         first_part = image_inner / unknowns
         gram = gram / unknowns

time: 253 us -> 269 us (1.063)
  blocking collectives: 91.9 us -> 112 us
    psum x2 -> x4, blocking collectives: 79.6 us -> 100 us  [the longest x2 77.1 us: by_each_axis(): return lax.psum(half, other)]
  transfers between devices with their start and end apart: 6 -> 6, of which waited for: 4 -> 5; matrix products, arithmetic and copies ran while one was open for 2% -> 2% of each run, Pallas kernels for 0% -> 0%
where the time goes in v1:
time: 269 us; the launch traced here: 268 us
  blocking collectives  112 us (42%)
  waiting for transfers between devices  69.5 us (26%)
  matrix products  41.1 us (15%)
  between operations  22.3 us (8%)
  local copies, waits for them, and re-layouts  10.9 us (4%)
  starting transfers between devices  7.88 us (3%)
  other arithmetic  4.73 us (2%)
    psum x2, blocking collectives, by_each_axis(): return lax.psum(half, other)  77.1 us
    unnamed x4, waiting for transfers between devices  62.1 us
    psum x2, blocking collectives, by_each_axis(): half = lax.psum(array_2, one)  23 us
    all_gather x2, blocking collectives, on_device(): whole_part = lax.all_gather(vectors, 'sub', axis=1, tiled=True)  11.9 us
    dot_general x2, matrix products, tile_products(): jnp.einsum('sij,sj->si', damping, picked_damp, preferred_element_type=jnp...  9.02 us
    ppermute x2, waiting for transfers between devices, padded(): after = lax.ppermute(initial, axis, down)  7.23 us
    dot_general x2, matrix products, tile_products(): jnp.einsum('sij,sj->si', stiffness, picked_stiff, preferred_element_type=...  6.71 us
  transfers between devices with their start and end apart: 6, of which 5 were waited for; matrix products, arithmetic and copies ran while one was open for 2% of the time, Pallas kernels for 0%

profile of v1, /device:TPU:0, one launch (start us, length us, event | category | flops | bytes accessed | tf_op | source)
XLA Modules:
  0.0 268.5 jit_solution(12291621375483048990)
XLA Ops:
  7.2 1.0 fusion.104
  8.5 0.2 slice_reduce_fusion.4
  8.7 2.7 %fusion.54 = f32[1,8192]{1,0:T(1,128)S(1)} fusion(f32[58,8192]{1,0:T(8,128)} %param.12, f32[58]{0:T(128)S(1)} %get-tuple-element.54), kind=kOutput, calls=%fused_computation.120 | convolution fusion | flops 5701632 | bytes 1933544 | tf_op jit(solution)/shard_map/dot_general | solution.py:84
  11.4 1.1 fusion.52
  12.6 6.5 %all_gather.6 = bf16[2,32768]{1,0:T(2,128)(2,1)S(1)} all-gather(bf16[2,8192]{1,0:T(2,128)(2,1)S(1)} %pad_maximum_fusion.8), channel_id=1, replica_groups=mesh['rows'=8,'sub'=4] {'sub'}, dimensions={1}, use_global_device_ids=true | all-gather | bytes 163840 | tf_op jit(solution)/shard_map/all_gather | solution.py:87
  19.1 3.9 %collective-permute-start = (bf16[2,32768]{1,0:T(2,128)(2,1)S(1)}, bf16[2,32768]{1,0:T(2,128)(2,1)S(1)}, u32[]{:S(2)}, u32[]{:S(2)}) collective-permute-start(bf16[2,32768]{1,0:T(2,128)(2,1)S(1)} %all_gather.6), channel_id=1, source_target_pairs={{0,4},{4,8},{8,12},{12,16},{16,20},{20,24},{24,28},{1,5},{5,9},{9,... | collective-permute-start | bytes 393224 | tf_op jit(solution)/shard_map/ppermute | solution.py:22
  23.1 1.3 collective-permute-start.1
  24.4 1.8 fusion.115
  27.1 3.4 %collective-permute-done.1 = bf16[2,32768]{1,0:T(2,128)(2,1)S(1)} collective-permute-done((bf16[2,32768]{1,0:T(2,128)(2,1)S(1)}, bf16[2,32768]{1,0:T(2,128)(2,1)S(1)}, u32[]{:S(2)}, u32[]{:S(2)}) %collective-permute-start.1) | collective-permute-done | bytes 131104 | tf_op jit(solution)/shard_map/ppermute | solution.py:23
  30.5 2.1 slice_reduce_fusion.2
  32.6 0.7 gather_fusion
  33.3 0.7 gather_fusion.1
  34.0 4.6 %fusion.6 = f32[128,1,128]{2,1,0:T(1,128)S(1)} fusion(bf16[1,1,128,128,128]{4,3,2,1,0:T(8,128)(2,1)} %param.8, bf16[128,128,1]{1,0,2:T(8,128)(2,1)S(1)} %bitcast.283), kind=kOutput, calls=%fused_computation.12 | convolution fusion | flops 4194304 | bytes 4292608 | tf_op jit(solution)/shard_map/sij,sj->si/dot_general | solution.py:54
  38.6 2.3 fusion.2
  40.9 0.9 convolution_bitcast_fusion.1
  41.9 0.6 dynamic-slice
  43.2 31.7 %all-reduce.13.cloned.1.call-done = f32[32768]{0:T(1024)} async-done(((f32[32768]{0:T(1024)}), f32[32768]{0:T(1024)}) %all-reduce.13.cloned.1.call-update) | async-done | bytes 131088
  74.9 1.4 multiply_reduce_fusion.1
  76.3 1.7 convolution_bitcast_fusion.23
  78.0 11.5 %all-reduce.9 = (f32[58,58]{1,0:T(8,128)S(1)}, f32[58]{0:T(128)S(1)}, f32[]{:T(128)}) all-reduce(f32[58,58]{1,0:T(8,128)S(1)} %fusion.115, f32[58]{0:T(128)S(1)} %convolution_bitcast_fusion.23, f32[]{:T(128)} %get-tuple-element.33), channel_id=1, replica_groups=mesh['rows'=8,'sub'=4] {'sub'}, use_global_device_ids=true, to_apply=%region_3.0 | all-reduce | flops 3423 | bytes 27384 | tf_op jit(solution)/shard_map/psum | solution.py:11
  89.5 38.5 %all-reduce.7 = (f32[58,58]{1,0:T(8,128)S(1)}, f32[58]{0:T(128)S(1)}, f32[]{:T(128)}) all-reduce(f32[58,58]{1,0:T(8,128)S(1)} %get-tuple-element.25, f32[58]{0:T(128)S(1)} %get-tuple-element.26, f32[]{:T(128)} %get-tuple-element.27), channel_id=1, replica_groups=mesh['rows'=8,'sub'=4] {'rows'}, use_global_device_ids=true, to_apply=%region_4.0 | all-reduce | flops 3423 | bytes 27384 | tf_op jit(solution)/shard_map/psum | solution.py:12
  128.0 0.8 multiply_reduce_fusion.3
  128.8 0.8 fusion.26
  131.6 0.2 convolution_bitcast_fusion.19
  131.8 0.2 fusion.22
  132.0 0.2 fusion.20
  132.1 0.2 fusion.21
  132.3 0.2 convolution_bitcast_fusion.16
  132.5 0.1 fusion.106
  132.6 0.8 multiply_reduce_fusion.6
  133.4 0.8 multiply_reduce_fusion.7
  134.2 1.1 fusion.76
  136.7 1.1 fusion.31
  137.8 1.1 fusion.30
  139.1 5.4 %all_gather.7 = bf16[2,32768]{1,0:T(2,128)(2,1)S(1)} all-gather(bf16[2,8192]{1,0:T(2,128)(2,1)S(1)} %pad_maximum_fusion.9), channel_id=1, replica_groups=mesh['rows'=8,'sub'=4] {'sub'}, dimensions={1}, use_global_device_ids=true | all-gather | bytes 163840 | tf_op jit(solution)/shard_map/all_gather | solution.py:87
  144.5 1.3 collective-permute-start.2
  145.8 1.3 collective-permute-start.3
  147.1 1.8 fusion.29
  149.6 3.9 %collective-permute-done.3 = bf16[2,32768]{1,0:T(2,128)(2,1)S(1)} collective-permute-done((bf16[2,32768]{1,0:T(2,128)(2,1)S(1)}, bf16[2,32768]{1,0:T(2,128)(2,1)S(1)}, u32[]{:S(2)}, u32[]{:S(2)}) %collective-permute-start.3) | collective-permute-done | bytes 131104 | tf_op jit(solution)/shard_map/ppermute | solution.py:23
  153.6 2.1 slice_reduce_fusion
  155.6 0.7 gather_fusion.3
  156.4 4.4 %fusion = f32[128,1,128]{2,1,0:T(1,128)S(1)} fusion(bf16[1,1,128,128,128]{4,3,2,1,0:T(8,128)(2,1)} %param.7, bf16[128,128,1]{1,0,2:T(8,128)(2,1)S(1)} %bitcast.286), kind=kOutput, calls=%fused_computation.6 | convolution fusion | flops 4194304 | bytes 4292608 | tf_op jit(solution)/shard_map/sij,sj->si/dot_general | solution.py:55
  160.8 0.7 gather_fusion.2
  161.5 4.4 %fusion.4 = f32[128,1,128]{2,1,0:T(1,128)S(1)} fusion(bf16[1,1,128,128,128]{4,3,2,1,0:T(8,128)(2,1)} %param.8, bf16[128,128,1]{1,0,2:T(8,128)(2,1)S(1)} %bitcast.285), kind=kOutput, calls=%fused_computation.10 | convolution fusion | flops 4194304 | bytes 4292608 | tf_op jit(solution)/shard_map/sij,sj->si/dot_general | solution.py:54
  166.0 0.9 convolution_bitcast_fusion
  167.0 30.4 %all-reduce.15.cloned.1.call-done = f32[32768]{0:T(1024)} async-done(((f32[32768]{0:T(1024)}), f32[32768]{0:T(1024)}) %all-reduce.15.cloned.1.call-update) | async-done | bytes 131088
  197.3 1.4 multiply_reduce_fusion
  198.7 1.7 convolution_bitcast_fusion.22
  200.4 11.5 %all-reduce.8 = (f32[59,59]{1,0:T(8,128)S(1)}, f32[59]{0:T(128)S(1)}, f32[]{:T(128)}) all-reduce(f32[59,59]{1,0:T(8,128)S(1)} %fusion.29, f32[59]{0:T(128)S(1)} %convolution_bitcast_fusion.22, f32[]{:T(128)} %get-tuple-element.31), channel_id=1, replica_groups=mesh['rows'=8,'sub'=4] {'sub'}, use_global_device_ids=true, to_apply=%region_13.0 | all-reduce | flops 3541 | bytes 28328 | tf_op jit(solution)/shard_map/psum | solution.py:11
  211.9 38.5 %all-reduce.6 = (f32[59,59]{1,0:T(8,128)S(1)}, f32[59]{0:T(128)S(1)}, f32[]{:T(128)}) all-reduce(f32[59,59]{1,0:T(8,128)S(1)} %get-tuple-element.22, f32[59]{0:T(128)S(1)} %get-tuple-element.23, f32[]{:T(128)} %get-tuple-element.24), channel_id=1, replica_groups=mesh['rows'=8,'sub'=4] {'rows'}, use_global_device_ids=true, to_apply=%region_14.0 | all-reduce | flops 3541 | bytes 28328 | tf_op jit(solution)/shard_map/psum | solution.py:12
  250.5 0.8 multiply_reduce_fusion.2
  251.3 0.8 fusion.27
  254.0 0.2 convolution_bitcast_fusion.9
  254.2 0.2 fusion.13
  254.4 0.2 fusion.12
  254.6 0.2 fusion.11
  254.8 0.2 convolution_bitcast_fusion.6
  254.9 0.1 fusion.105
  255.1 0.8 multiply_reduce_fusion.5
  255.9 0.8 multiply_reduce_fusion.4
  256.6 1.1 fusion.28
  259.5 0.7 copy.32
  260.3 0.7 pad_maximum_fusion.6
  261.0 0.6 pad_maximum_fusion.10
  (56 shorter events, 2.3 us)
Async XLA Ops:
  7.2 4.2 %copy-start = (f32[58,8192]{1,0:T(8,128)S(1)}, f32[58,8192]{1,0:T(8,128)}, u32[]{:S(2)}) copy-start(f32[58,8192]{1,0:T(8,128)} %param.12) | copy-start | bytes 5701636
  7.2 67.7 %all-reduce.13.cloned.1.call-start = ((), (), s32[]{:S(2)}) async-start(), calls=%async_computation | async-start | bytes 262144
  19.1 7.0 %copy-start.3 = (s32[1,1,2,128]{3,2,1,0:T(2,128)S(1)}, s32[1,1,2,128]{3,2,1,0:T(2,128)}, u32[]{:S(2)}) copy-start(s32[1,1,2,128]{3,2,1,0:T(2,128)} %param.9) | copy-start | bytes 3076
  19.1 7.7 %collective-permute-start = (bf16[2,32768]{1,0:T(2,128)(2,1)S(1)}, bf16[2,32768]{1,0:T(2,128)(2,1)S(1)}, u32[]{:S(2)}, u32[]{:S(2)}) collective-permute-start(bf16[2,32768]{1,0:T(2,128)(2,1)S(1)} %all_gather.6), channel_id=1, source_target_pairs={{0,4},{4,8},{8,12},{12,16},{16,20},{20,24},{24,28},{1,5},{5,9},{9,... | collective-permute-start | bytes 393224 | tf_op jit(solution)/shard_map/ppermute | solution.py:22
  23.1 7.4 %collective-permute-start.1 = (bf16[2,32768]{1,0:T(2,128)(2,1)S(1)}, bf16[2,32768]{1,0:T(2,128)(2,1)S(1)}, u32[]{:S(2)}, u32[]{:S(2)}) collective-permute-start(bf16[2,32768]{1,0:T(2,128)(2,1)S(1)} %all_gather.6), channel_id=1, source_target_pairs={{4,0},{8,4},{12,8},{16,12},{20,16},{24,20},{28,24},{5,1},{9,5},{13... | collective-permute-start | bytes 393224 | tf_op jit(solution)/shard_map/ppermute | solution.py:23
  34.0 4.6 %copy-start.1 = (bf16[1,1,128,128,128]{4,3,2,1,0:T(8,128)(2,1)S(1)}, bf16[1,1,128,128,128]{4,3,2,1,0:T(8,128)(2,1)}, u32[]{:S(2)}) copy-start(bf16[1,1,128,128,128]{4,3,2,1,0:T(8,128)(2,1)} %param.7) | copy-start | bytes 12582916
  38.6 3.3 %copy-start.4 = (u32[32]{0:T(128)S(1)}, u32[32]{0:T(128)}, u32[]{:S(2)}) copy-start(u32[32]{0:T(128)} %constant.43) | copy-start | bytes 388
  38.6 36.3 %copy-start.2 = (f32[8192]{0:T(1024)S(1)}, f32[8192]{0:T(1024)}, u32[]{:S(2)}) copy-start(f32[8192]{0:T(1024)} %param.10) | copy-start | bytes 98308
  41.8 155.5 %all-reduce.15.cloned.1.call-start = ((), (), s32[]{:S(2)}) async-start(), calls=%async_computation.1 | async-start | bytes 262144
  144.5 4.9 %collective-permute-start.2 = (bf16[2,32768]{1,0:T(2,128)(2,1)S(1)}, bf16[2,32768]{1,0:T(2,128)(2,1)S(1)}, u32[]{:S(2)}, u32[]{:S(2)}) collective-permute-start(bf16[2,32768]{1,0:T(2,128)(2,1)S(1)} %all_gather.7), channel_id=1, source_target_pairs={{0,4},{4,8},{8,12},{12,16},{16,20},{20,24},{24,28},{1,5},{5,9},{9,... | collective-permute-start | bytes 393224 | tf_op jit(solution)/shard_map/ppermute | solution.py:22
  145.8 7.6 %collective-permute-start.3 = (bf16[2,32768]{1,0:T(2,128)(2,1)S(1)}, bf16[2,32768]{1,0:T(2,128)(2,1)S(1)}, u32[]{:S(2)}, u32[]{:S(2)}) collective-permute-start(bf16[2,32768]{1,0:T(2,128)(2,1)S(1)} %all_gather.7), channel_id=1, source_target_pairs={{4,0},{8,4},{12,8},{16,12},{20,16},{24,20},{28,24},{5,1},{9,5},{13... | collective-permute-start | bytes 393224 | tf_op jit(solution)/shard_map/ppermute | solution.py:23
Sparse Core Ops, SparseCore 0:
  41.9 32.9 all-reduce.12
  167.0 30.2 all-reduce.14
